TPU v7x, 32 devices: a whole 2x2x4 slice. The times are simulated.
32 devices in a mesh: groups: 2 (over x), row: 16 (over z, y, core).
Axes of the slice: x: 2, y: 2, z: 4, core: 2. Of those that a mesh axis runs over, the one named last changes fastest.
Arguments:
- design_matrix: bfloat16 [1024, 65536], P('groups', 'row'), parts along dimension 0, may hold values from -0.0546875 to 0.0546875
- targets: float32 [1024, 128], P(('groups', 'row')), parts along dimension 0, may hold values from -24 to 24
- linear: float32 [131072, 128], P(('groups', 'row')), parts along dimension 0, may hold values from -24 to 24
- diagonal: float32 [131072], P(('groups', 'row')), parts along dimension 0, may hold values from 0.1 to 2
- lower_code: int32 [131072, 128], P(('groups', 'row')), parts along dimension 0, may hold values from -192 to -17
- upper_code: int32 [131072, 128], P(('groups', 'row')), parts along dimension 0, may hold values from 16 to 191
Outputs:
- box_iterate: float32 [131072, 128], P(('groups', 'row')), parts along dimension 0
- scaled_dual: float32 [131072, 128], P(('groups', 'row')), parts along dimension 0
There are 2 independent parts, one for each index of `groups`. A program takes and returns all parts, laid end to end along the dimension named above; each array names one. Nothing has to cross between parts.
All inputs are finite; a program needn't handle non-finite values.
Results may differ from a plain program's by a relative error of at most 0.00033.
Values may be sent and summed in bfloat16 or wider, within the bound.
No kernel may reach another device: no remote copies, remote signals or barrier semaphores. Data moves between devices by JAX's collectives and lax.ppermute only.
A program may use at most 128 MiB of HBM per device.

v0:
```python
import jax
import jax.numpy as jnp
from jax import lax
from jax.sharding import PartitionSpec as P

ITERS = 4
rho_plus_lip = 7.0


def solve_small(matrix, rhs):
    count = len(rhs)
    table = [list(line) for line in matrix]
    right = list(rhs)
    for p in range(count):
        for i in range(p + 1, count):
            factor = table[i][p] / table[p][p]
            for j in range(p, count):
                table[i][j] = table[i][j] - factor * table[p][j]
            right[i] = right[i] - factor * right[p]
    result = [None] * count
    for i in reversed(range(count)):
        total = right[i]
        for j in range(i + 1, count):
            total = total - table[i][j] * result[j]
        result[i] = total / table[i][i]
    return result


def mix_weights(gram):
    count = len(gram)
    trace = gram[0][0]
    for i in range(1, count):
        trace = trace + gram[i][i]
    shift = 0.01 * trace / count + 1e-06
    matrix = [[gram[i][j] + (shift if i == j else 0.0) for j in range(count)] for i in range(count)]
    solved = solve_small(matrix, [jnp.ones_like(trace)] * count)
    total = solved[0]
    for i in range(1, count):
        total = total + solved[i]
    return [item / total for item in solved]


def apply_map(design_matrix, misfit, z, u, linear, diag, step_size, lower, upper):
    gradient = lax.dot_general(
        design_matrix, misfit, (((0,), (0,)), ((), ())), preferred_element_type=jnp.float32
    )
    point = z - u
    gradient = gradient + diag * point + linear
    moved = point - step_size * gradient
    boxed = jnp.clip(moved + u, lower, upper)
    return (boxed, u + moved - boxed)


def per_device(design_matrix, targets, linear, diagonal, lower_code, upper_code):
    lower = lower_code.astype(jnp.float32) / 64.0
    upper = upper_code.astype(jnp.float32) / 64.0
    diag = diagonal[:, None]
    step_size = 1.0 / (rho_plus_lip + diag)
    z = jnp.zeros(linear.shape, jnp.float32)
    u = z
    mapped = []
    change = []
    gram = {}
    fresh = []
    for iteration in range(ITERS):
        if iteration == 0:
            misfit = (-targets).astype(jnp.bfloat16)
        else:
            product = lax.psum_scatter(
                jnp.dot(
                    design_matrix, (z - u).astype(jnp.bfloat16), preferred_element_type=jnp.float32
                ),
                "row",
                scatter_dimension=0,
                tiled=True,
            )
            misfit = (product - targets).astype(jnp.bfloat16)
        misfit = lax.all_gather(misfit, "row", axis=0, tiled=True)
        boxed, scaled = apply_map(
            design_matrix, misfit, z, u, linear, diag, step_size, lower, upper
        )
        mapped.append((boxed, scaled))
        change.append((boxed - z, scaled - u))
        for i in range(iteration + 1):
            fresh.append(
                (
                    (i, iteration),
                    jnp.sum(
                        change[i][0] * change[iteration][0] + change[i][1] * change[iteration][1],
                        axis=0,
                    ),
                )
            )
        if iteration == 0:
            z, u = (boxed, scaled)
            continue
        partial = jnp.stack([item for _, item in fresh])
        whole = jnp.sum(lax.all_gather(partial, "row", axis=0), axis=0)
        for k, (pair, _) in enumerate(fresh):
            gram[pair] = whole[k]
        fresh = []
        count = iteration + 1
        alpha = mix_weights(
            [[gram[min(i, j), max(i, j)] for j in range(count)] for i in range(count)]
        )
        z = alpha[0][None, :] * mapped[0][0]
        u = alpha[0][None, :] * mapped[0][1]
        for i in range(1, count):
            z = z + alpha[i][None, :] * mapped[i][0]
            u = u + alpha[i][None, :] * mapped[i][1]
        z = jnp.clip(z, lower, upper)
    return (z, u)


def solution(mesh):
    in_specs = (
        P("groups", "row"),
        P(("groups", "row"), None),
        P(("groups", "row"), None),
        P(("groups", "row")),
        P(("groups", "row"), None),
        P(("groups", "row"), None),
    )
    out_specs = (P(("groups", "row"), None), P(("groups", "row"), None))
    return jax.shard_map(
        per_device, mesh=mesh, in_specs=in_specs, out_specs=out_specs, check_vma=False
    )
```

profile of v0, /device:TPU:0, one launch (start us, length us, event | category | flops | bytes accessed | tf_op | source)
XLA Modules:
  0.0 378.7 jit_solution(17872735415210531985)
XLA Ops:
  7.2 0.0 reduce-scatter.4.cloned.1.call-start
  7.2 0.7 negate_convert_fusion
  7.9 0.7 add_divide_fusion
  8.7 23.5 %all_gather.30 = bf16[512,128]{1,0:T(8,128)(2,1)S(1)} all-gather(bf16[32,128]{1,0:T(8,128)(2,1)S(1)} %negate_convert_fusion), channel_id=1, replica_groups=mesh['groups'=2,'row'=16] {'row'}, dimensions={0}, use_global_device_ids=true | all-gather | bytes 139264 | tf_op jit(solution)/shard_map/all_gather | solution.py:78
  32.1 6.4 %fusion.52 = (f32[4096,128]{1,0:T(8,128)S(1)}, f32[4096,128]{1,0:T(8,128)}, f32[4096,128]{1,0:T(8,128)S(1)}) fusion(s32[4096,128]{1,0:T(8,128)} %param.10, s32[4096,128]{1,0:T(8,128)} %param.11, f32[4096,128]{1,0:T(8,128)} %param.8, f32[4096]{0:T(1024)S(1)} %get-tuple-element.64, bf16[512,4096]{1,0:T(8,128)(2,1)} %param.6, ...), kind=kOutput, calls=%fused_computation.132 | convolution fusion | flops 543162368 | bytes 16941056 | tf_op jit(solution)/shard_map/dot_general | solution.py:44
  38.5 1.3 copy-done.6
  39.8 1.9 convolution_bitcast_fusion.5
  41.8 0.0 reduce-scatter.4.cloned.1.call-update
  41.8 0.0 reduce-scatter.6.cloned.1.call-start
  41.8 53.1 %reduce-scatter.4.cloned.1.call-done = f32[32,128]{1,0:T(8,128)} async-done(((f32[512,128]{1,0:T(8,128)}), f32[32,128]{1,0:T(8,128)}) %reduce-scatter.4.cloned.1.call-update) | async-done | bytes 16400 | tf_op jit(solution)/shard_map/reduce_scatter | solution.py:69
  94.9 0.7 subtract_convert_fusion.2
  95.6 19.7 %all_gather.31 = bf16[512,128]{1,0:T(8,128)(2,1)S(1)} all-gather(bf16[32,128]{1,0:T(8,128)(2,1)S(1)} %subtract_convert_fusion.2), channel_id=1, replica_groups=mesh['groups'=2,'row'=16] {'row'}, dimensions={0}, use_global_device_ids=true | all-gather | bytes 139264 | tf_op jit(solution)/shard_map/all_gather | solution.py:78
  115.4 8.5 %add_reduce_fusion.9 = (f32[128]{0:T(128)S(1)}, f32[128]{0:T(128)S(1)}, f32[128]{0:T(128)S(1)}, f32[4096,128]{1,0:T(8,128)}, f32[4096,128]{1,0:T(8,128)}, /*index=5*/f32[4096,128]{1,0:T(8,128)}) fusion(f32[4096,128]{1,0:T(8,128)} %get-tuple-element.57, f32[4096,128]{1,0:T(8,128)S(1)} %get-tuple-element.58, s32[4096,128]{1,0:T(8,128)} %param.10, ...), kind=kOutput, calls=%fused_computation.40 | convolution fusion | flops 551026304 | bytes 23234048 | tf_op jit(solution)/shard_map/dot_general | solution.py:44
  123.9 17.5 %all-gather.3 = f32[16,3,128]{2,1,0:T(4,128)S(1)} all-gather(f32[1,3,128]{2,1,0:T(4,128)S(1)} %maximum_bitcast_fusion), channel_id=2, replica_groups=mesh['groups'=2,'row'=16] {'row'}, dimensions={0}, use_global_device_ids=true | all-gather | bytes 26112 | tf_op jit(solution)/shard_map/all_gather | solution.py:98
  141.5 6.9 %convolution_bitcast_fusion.4 = f32[512,128]{1,0:T(8,128)} fusion(bf16[512,4096]{1,0:T(8,128)(2,1)} %param.6, f32[4096,128]{1,0:T(8,128)} %get-tuple-element.70, f32[128]{0:T(128)S(1)} %fusion.24, f32[4096,128]{1,0:T(8,128)S(1)} %get-tuple-element.58, f32[128]{0:T(128)S(1)} %get-tuple-element.48, s32[4096,128]{1,0:T(8,128)} %param.10, ...), kind=kOutput, calls=%fused_computation.45 | convolution fusion | flops 545783808 | bytes 14943232 | tf_op jit(solution)/shard_map/dot_general | solution.py:70
  148.4 0.0 reduce-scatter.8.cloned.1.call-start
  148.5 54.2 %reduce-scatter.6.cloned.1.call-done = f32[32,128]{1,0:T(8,128)} async-done(((f32[512,128]{1,0:T(8,128)}), f32[32,128]{1,0:T(8,128)}) %reduce-scatter.6.cloned.1.call-update) | async-done | bytes 16400 | tf_op jit(solution)/shard_map/reduce_scatter | solution.py:69
  202.7 0.7 subtract_convert_fusion.1
  203.4 19.8 %all_gather.34 = bf16[512,128]{1,0:T(8,128)(2,1)S(1)} all-gather(bf16[32,128]{1,0:T(8,128)(2,1)S(1)} %subtract_convert_fusion.1), channel_id=1, replica_groups=mesh['groups'=2,'row'=16] {'row'}, dimensions={0}, use_global_device_ids=true | all-gather | bytes 139264 | tf_op jit(solution)/shard_map/all_gather | solution.py:78
  223.2 10.1 %add_reduce_fusion.6 = (f32[128]{0:T(128)S(1)}, f32[128]{0:T(128)S(1)}, f32[128]{0:T(128)S(1)}, f32[4096,128]{1,0:T(8,128)}, f32[4096,128]{1,0:T(8,128)}, /*index=5*/f32[4096,128]{1,0:T(8,128)}) fusion(f32[4096,128]{1,0:T(8,128)} %get-tuple-element.57, f32[4096,128]{1,0:T(8,128)S(1)} %get-tuple-element.58, f32[4096,128]{1,0:T(8,128)} %get-tuple-element.55, ...), kind=kOutput, calls=%fused_computation.33 | convolution fusion | flops 557317760 | bytes 27429376 | tf_op jit(solution)/shard_map/dot_general | solution.py:44
  233.3 17.7 %all-gather.4 = f32[16,3,128]{2,1,0:T(4,128)S(1)} all-gather(f32[1,3,128]{2,1,0:T(4,128)S(1)} %maximum_bitcast_fusion.1), channel_id=3, replica_groups=mesh['groups'=2,'row'=16] {'row'}, dimensions={0}, use_global_device_ids=true | all-gather | bytes 26112 | tf_op jit(solution)/shard_map/all_gather | solution.py:98
  251.1 7.1 %fusion.33 = (f32[4096,128]{1,0:T(8,128)S(1)}, f32[4096,128]{1,0:T(8,128)}) fusion(f32[128]{0:T(128)S(1)} %get-tuple-element.69, f32[128]{0:T(128)S(1)} %get-tuple-element.68, f32[4096,128]{1,0:T(8,128)S(1)} %get-tuple-element.58, f32[128]{0:T(128)S(1)} %get-tuple-element.36, s32[4096,128]{1,0:T(8,128)} %param.10, s32[4096,128]{1,0:T(8,128)} %param.11, ...), kind=kLoop, calls=%fused_computation.112 | loop fusion | flops 12058624 | bytes 16778752 | tf_op jit(solution)/shard_map/sub | solution.py:47
  258.2 1.3 copy-done.5
  259.5 2.0 convolution_bitcast_fusion.3
  261.5 54.2 %reduce-scatter.8.cloned.1.call-done = f32[32,128]{1,0:T(8,128)} async-done(((f32[512,128]{1,0:T(8,128)}), f32[32,128]{1,0:T(8,128)}) %reduce-scatter.8.cloned.1.call-update) | async-done | bytes 16400 | tf_op jit(solution)/shard_map/reduce_scatter | solution.py:69
  315.8 0.7 subtract_convert_fusion
  316.5 19.7 %all_gather.37 = bf16[512,128]{1,0:T(8,128)(2,1)S(1)} all-gather(bf16[32,128]{1,0:T(8,128)(2,1)S(1)} %subtract_convert_fusion), channel_id=1, replica_groups=mesh['groups'=2,'row'=16] {'row'}, dimensions={0}, use_global_device_ids=true | all-gather | bytes 139264 | tf_op jit(solution)/shard_map/all_gather | solution.py:78
  336.3 9.4 %fusion.22 = (f32[4096,128]{1,0:T(8,128)S(1)}, f32[4096,128]{1,0:T(8,128)S(1)}, f32[4096,128]{1,0:T(8,128)}) fusion(s32[4096,128]{1,0:T(8,128)} %param.10, s32[4096,128]{1,0:T(8,128)} %param.11, f32[128]{0:T(128)S(1)} %get-tuple-element.69, f32[128]{0:T(128)S(1)} %get-tuple-element.68, f32[4096,128]{1,0:T(8,128)S(1)} %get-tuple-element.58, ...), kind=kOutput, calls=%fused_computation.51 | convolution fusion | flops 550502400 | bytes 27428352 | tf_op jit(solution)/shard_map/dot_general | solution.py:44
  345.7 0.8 copy-done.8
  346.5 1.1 add_reduce_fusion.3
  347.6 17.5 %all-gather.5 = f32[16,4,128]{2,1,0:T(4,128)S(1)} all-gather(f32[1,4,128]{2,1,0:T(4,128)S(1)} %maximum_bitcast_fusion.2), channel_id=4, replica_groups=mesh['groups'=2,'row'=16] {'row'}, dimensions={0}, use_global_device_ids=true | all-gather | bytes 34816 | tf_op jit(solution)/shard_map/all_gather | solution.py:98
  365.3 6.9 %multiply_add_fusion = (f32[4096,128]{1,0:T(8,128)}, f32[4096,128]{1,0:T(8,128)}) fusion(f32[4096,128]{1,0:T(8,128)} %get-tuple-element.57, f32[128]{0:T(128)S(1)} %get-tuple-element.67, f32[128]{0:T(128)S(1)} %get-tuple-element.66, f32[128]{0:T(128)S(1)} %get-tuple-element.65, f32[128]{0:T(128)S(1)} %get-tuple-element.12, ...), kind=kLoop, calls=%fused_computation.22 | loop fusion | flops 15204352 | bytes 18876416 | tf_op jit(solution)/shard_map/add | solution.py:110
  (38 shorter events, 0.4 us)
Async XLA Ops:
  7.2 87.7 %reduce-scatter.4.cloned.1.call-start = ((), (), s32[]{:S(2)}) async-start(), calls=%async_computation.3 | async-start | bytes 278528 | tf_op jit(solution)/shard_map/reduce_scatter | solution.py:69
  32.1 7.7 %copy-start = (bf16[512,4096]{1,0:T(8,128)(2,1)S(1)}, bf16[512,4096]{1,0:T(8,128)(2,1)}, u32[]{:S(2)}) copy-start(bf16[512,4096]{1,0:T(8,128)(2,1)} %param.6) | copy-start | bytes 12582916
  38.5 1.3 copy-start.6
  39.8 55.1 %copy-start.10 = (f32[32,128]{1,0:T(8,128)S(1)}, f32[32,128]{1,0:T(8,128)}, u32[]{:S(2)}) copy-start(f32[32,128]{1,0:T(8,128)} %param.7) | copy-start | bytes 49156
  39.8 75.6 %copy-start.9 = (f32[4096]{0:T(1024)S(1)}, f32[4096]{0:T(1024)}, u32[]{:S(2)}) copy-start(f32[4096]{0:T(1024)} %param.9) | copy-start | bytes 49156
  41.8 160.9 %reduce-scatter.6.cloned.1.call-start = ((), (), s32[]{:S(2)}) async-start(), calls=%async_computation.4 | async-start | bytes 278528 | tf_op jit(solution)/shard_map/reduce_scatter | solution.py:69
  148.4 167.4 %reduce-scatter.8.cloned.1.call-start = ((), (), s32[]{:S(2)}) async-start(), calls=%async_computation.5 | async-start | bytes 278528 | tf_op jit(solution)/shard_map/reduce_scatter | solution.py:69
  251.1 8.5 %copy-start.1 = (bf16[512,4096]{1,0:T(8,128)(2,1)S(1)}, bf16[512,4096]{1,0:T(8,128)(2,1)}, u32[]{:S(2)}) copy-start(bf16[512,4096]{1,0:T(8,128)(2,1)} %param.6) | copy-start | bytes 12582916
  258.2 1.3 copy-start.5
  336.3 9.4 %copy-start.2 = (f32[4096,128]{1,0:T(8,128)S(1)}, f32[4096,128]{1,0:T(8,128)}, u32[]{:S(2)}) copy-start(f32[4096,128]{1,0:T(8,128)} %get-tuple-element.57) | copy-start | bytes 6291460
  336.3 9.4 %copy-start.3 = (f32[4096,128]{1,0:T(8,128)S(1)}, f32[4096,128]{1,0:T(8,128)}, u32[]{:S(2)}) copy-start(f32[4096,128]{1,0:T(8,128)} %get-tuple-element.54) | copy-start | bytes 6291460
  336.3 9.4 %copy-start.4 = (f32[4096,128]{1,0:T(8,128)S(1)}, f32[4096,128]{1,0:T(8,128)}, u32[]{:S(2)}) copy-start(f32[4096,128]{1,0:T(8,128)} %get-tuple-element.55) | copy-start | bytes 6291460
  336.3 9.5 %copy-start.7 = (f32[4096,128]{1,0:T(8,128)S(1)}, f32[4096,128]{1,0:T(8,128)}, u32[]{:S(2)}) copy-start(f32[4096,128]{1,0:T(8,128)} %get-tuple-element.46) | copy-start | bytes 6291460
  336.3 10.3 %copy-start.8 = (f32[4096,128]{1,0:T(8,128)S(1)}, f32[4096,128]{1,0:T(8,128)}, u32[]{:S(2)}) copy-start(f32[4096,128]{1,0:T(8,128)} %get-tuple-element.47) | copy-start | bytes 6291460
Sparse Core Ops, SparseCore 0:
  41.9 52.9 reduce-scatter.3
  148.5 54.1 reduce-scatter.5
  261.7 54.0 reduce-scatter.7
where the time goes:
time: 379 us
  waiting for transfers between devices  162 us (43%)
  blocking collectives  135 us (36%)
  matrix products  45.2 us (12%)
  other arithmetic  19.1 us (5%)
  between operations  13.9 us (4%)
    reduce_scatter x3, waiting for transfers between devices, per_device(): lax.psum_scatter(jnp.dot(design_matrix, (z - u).astype(jnp.bfloat16), pre...  162 us
    all_gather x4, blocking collectives, per_device(): misfit = lax.all_gather(misfit, 'row', axis=0, tiled=True)  82.7 us
    all_gather x3, blocking collectives, per_device(): whole = jnp.sum(lax.all_gather(partial, 'row', axis=0), axis=0)  52.7 us
    dot_general x4, matrix products, apply_map(): lax.dot_general(design_matrix, misfit, (((0,), (0,)), ((), ())), preferre...  34.4 us
    dot_general x3, matrix products, per_device(): jnp.dot(design_matrix, (z - u).astype(jnp.bfloat16), preferred_element_ty...  10.8 us
  transfers between devices with their start and end apart: 3, of which 3 were waited for; matrix products, arithmetic and copies ran while one was open for 0% of the time, Pallas kernels for 0%

commit v1 on v0

--- a/solution.py
+++ b/solution.py
@@ -75,7 +75,14 @@
                 tiled=True,
             )
             misfit = (product - targets).astype(jnp.bfloat16)
-        misfit = lax.all_gather(misfit, "row", axis=0, tiled=True)
+        ring = [misfit]
+        for hop in range(15):
+            ring.append(lax.ppermute(ring[-1], "row", [(dev, (dev + 1) % 16) for dev in range(16)]))
+        misfit = jnp.roll(
+            jnp.concatenate(ring[::-1], axis=0),
+            (lax.axis_index("row") + 1) * ring[0].shape[0],
+            axis=0,
+        )
         boxed, scaled = apply_map(
             design_matrix, misfit, z, u, linear, diag, step_size, lower, upper
         )

time: 379 us -> 676 us (1.78)
  waiting for transfers between devices: 162 us -> 519 us
  blocking collectives: 135 us -> 51.8 us
  local copies, waits for them, and re-layouts: 3.48 us -> 21.9 us
    ppermute x0 -> x60, waiting for transfers between devices: none -> 353 us  [per_device(): lax.ppermute(ring[-1], 'row', [(dev, (dev + 1) % 16) for dev in range(16)])]
    unnamed x3 -> x6, waiting for transfers between devices: 0.05 us -> 166 us
    reduce_scatter x3 -> x0, waiting for transfers between devices: 162 us -> none  [per_device(): lax.psum_scatter(jnp.dot(design_matrix, (z - u).astype(jnp.bfloat16), pre...]
    all_gather x4 -> x0, blocking collectives: 82.7 us -> none  [per_device(): misfit = lax.all_gather(misfit, 'row', axis=0, tiled=True)]
    unnamed x22 -> x53, local copies, waits for them, and re-layouts: 3.48 us -> 21.3 us
  transfers between devices with their start and end apart: 3 -> 63, of which waited for: 3 -> 62; matrix products, arithmetic and copies ran while one was open for 0% -> 1% of each run, Pallas kernels for 0% -> 0%
where the time goes in v1:
time: 676 us; the launch traced here: 675 us
  waiting for transfers between devices  519 us (77%)
  blocking collectives  51.8 us (8%)
  matrix products  49.8 us (7%)
  local copies, waits for them, and re-layouts  21.9 us (3%)
  other arithmetic  17.7 us (3%)
  between operations  14.1 us (2%)
    ppermute x60, waiting for transfers between devices, per_device(): lax.ppermute(ring[-1], 'row', [(dev, (dev + 1) % 16) for dev in range(16)])  353 us
    unnamed x6, waiting for transfers between devices  166 us
    all_gather x3, blocking collectives, per_device(): whole = jnp.sum(lax.all_gather(partial, 'row', axis=0), axis=0)  51.8 us
    dot_general x4, matrix products, apply_map(): lax.dot_general(design_matrix, misfit, (((0,), (0,)), ((), ())), preferre...  40.3 us
    unnamed x53, local copies, waits for them, and re-layouts  21.3 us
  transfers between devices with their start and end apart: 63, of which 62 were waited for; matrix products, arithmetic and copies ran while one was open for 1% of the time, Pallas kernels for 0%

profile of v1, /device:TPU:0, one launch (start us, length us, event | category | flops | bytes accessed | tf_op | source)
XLA Modules:
  0.0 675.5 jit_solution(9387571026774067223)
XLA Ops:
  8.4 6.3 collective-permute-done
  98.4 7.5 %fusion.69 = (f32[4096,128]{0,1:T(8,128)S(1)}, f32[4096,128]{0,1:T(8,128)}, f32[4096,128]{0,1:T(8,128)}) fusion(s32[4096,128]{0,1:T(8,128)S(1)} %copy.20, s32[4096,128]{0,1:T(8,128)} %copy.19, f32[4096,128]{0,1:T(8,128)} %copy.21, f32[4096]{0:T(1024)S(1)} %get-tuple-element.69, bf16[512,4096]{1,0:T(8,128)(2,1)} %param.8, s32[]{:T(128)S(6)} %select_n.17, ...), kind=kOutput, calls=%fused_computation.169 | convolution fusion | flops 543424512 | bytes 16941060 | tf_op jit(solution)/shard_map/dot_general | solution.py:44
  109.9 57.4 %reduce-scatter.10.cloned.1.call-done = f32[32,128]{1,0:T(8,128)} async-done(((f32[512,128]{1,0:T(8,128)}), f32[32,128]{1,0:T(8,128)}) %reduce-scatter.10.cloned.1.call-update) | async-done | bytes 16400
  174.1 6.0 collective-permute-done.16
  180.2 6.0 collective-permute-done.17
  186.2 6.0 collective-permute-done.18
  192.3 6.0 collective-permute-done.19
  198.3 6.0 collective-permute-done.20
  204.3 6.0 collective-permute-done.21
  210.4 6.0 collective-permute-done.22
  216.4 6.0 collective-permute-done.23
  222.4 6.0 collective-permute-done.24
  228.5 6.0 collective-permute-done.25
  234.5 6.0 collective-permute-done.26
  240.6 6.0 collective-permute-done.27
  258.9 10.4 %add_reduce_fusion.9 = (f32[128]{0:T(128)S(1)}, f32[128]{0:T(128)S(1)}, f32[128]{0:T(128)S(1)}, f32[4096,128]{0,1:T(8,128)}, f32[4096,128]{0,1:T(8,128)}, /*index=5*/f32[4096,128]{0,1:T(8,128)}) fusion(f32[4096,128]{0,1:T(8,128)} %get-tuple-element.62, f32[4096,128]{0,1:T(8,128)} %get-tuple-element.63, s32[4096,128]{0,1:T(8,128)S(1)} %copy.20, ...), kind=kOutput, calls=%fused_computation.41 | convolution fusion | flops 551288448 | bytes 23234052 | tf_op jit(solution)/shard_map/dot_general | solution.py:44
  269.4 17.4 %all-gather.3 = f32[16,3,128]{2,1,0:T(4,128)S(1)} all-gather(f32[1,3,128]{2,1,0:T(4,128)S(1)} %maximum_bitcast_fusion), channel_id=2, replica_groups=mesh['groups'=2,'row'=16] {'row'}, dimensions={0}, use_global_device_ids=true | all-gather | bytes 26112 | tf_op jit(solution)/shard_map/all_gather | solution.py:105
  286.8 6.4 convolution_bitcast_fusion.4
  294.2 54.5 %reduce-scatter.12.cloned.1.call-done = f32[32,128]{1,0:T(8,128)} async-done(((f32[512,128]{1,0:T(8,128)}), f32[32,128]{1,0:T(8,128)}) %reduce-scatter.12.cloned.1.call-update) | async-done | bytes 16400
  379.7 6.0 collective-permute-done.35
  391.8 6.0 collective-permute-done.37
  422.0 6.0 collective-permute-done.42
  440.4 12.3 %add_reduce_fusion.6 = (f32[128]{0:T(128)S(1)}, f32[128]{0:T(128)S(1)}, f32[128]{0:T(128)S(1)}, f32[4096,128]{0,1:T(8,128)}, f32[4096,128]{0,1:T(8,128)}, /*index=5*/f32[4096,128]{0,1:T(8,128)}) fusion(f32[4096,128]{0,1:T(8,128)} %get-tuple-element.62, f32[4096,128]{0,1:T(8,128)} %get-tuple-element.63, f32[4096,128]{0,1:T(8,128)} %get-tuple-element.60, ...), kind=kOutput, calls=%fused_computation.34 | convolution fusion | flops 557579904 | bytes 27429380 | tf_op jit(solution)/shard_map/dot_general | solution.py:44
  452.7 17.2 %all-gather.4 = f32[16,3,128]{2,1,0:T(4,128)S(1)} all-gather(f32[1,3,128]{2,1,0:T(4,128)S(1)} %maximum_bitcast_fusion.1), channel_id=3, replica_groups=mesh['groups'=2,'row'=16] {'row'}, dimensions={0}, use_global_device_ids=true | all-gather | bytes 26112 | tf_op jit(solution)/shard_map/all_gather | solution.py:105
  470.0 7.3 %fusion.50 = (f32[4096,128]{0,1:T(8,128)S(1)}, f32[4096,128]{0,1:T(8,128)}) fusion(f32[128]{0:T(128)S(1)} %get-tuple-element.74, f32[128]{0:T(128)S(1)} %get-tuple-element.73, f32[4096,128]{0,1:T(8,128)} %get-tuple-element.63, f32[128]{0:T(128)S(1)} %get-tuple-element.41, s32[4096,128]{0,1:T(8,128)S(1)} %copy.20, s32[4096,128]{0,1:T(8,128)} %copy.19, ...), kind=kLoop, calls=%fused_computation.149 | loop fusion | flops 12058624 | bytes 16778752 | tf_op jit(solution)/shard_map/sub | solution.py:47
  481.1 54.5 %reduce-scatter.14.cloned.1.call-done = f32[32,128]{1,0:T(8,128)} async-done(((f32[512,128]{1,0:T(8,128)}), f32[32,128]{1,0:T(8,128)}) %reduce-scatter.14.cloned.1.call-update) | async-done | bytes 16400
  548.6 6.0 collective-permute-done.47
  578.7 6.0 collective-permute-done.52
  590.8 6.0 collective-permute-done.54
  627.3 10.0 %fusion.31 = (f32[4096,128]{0,1:T(8,128)S(1)}, f32[4096,128]{0,1:T(8,128)S(1)}, f32[4096,128]{0,1:T(8,128)}) fusion(s32[4096,128]{0,1:T(8,128)S(1)} %copy.20, s32[4096,128]{0,1:T(8,128)} %copy.19, f32[128]{0:T(128)S(1)} %get-tuple-element.74, f32[128]{0:T(128)S(1)} %get-tuple-element.73, f32[4096,128]{0,1:T(8,128)} %get-tuple-element.63, ...), kind=kOutput, calls=%fused_computation.67 | convolution fusion | flops 550764544 | bytes 27428356 | tf_op jit(solution)/shard_map/dot_general | solution.py:44
  639.7 17.2 %all-gather.5 = f32[16,4,128]{2,1,0:T(4,128)S(1)} all-gather(f32[1,4,128]{2,1,0:T(4,128)S(1)} %maximum_bitcast_fusion.2), channel_id=4, replica_groups=mesh['groups'=2,'row'=16] {'row'}, dimensions={0}, use_global_device_ids=true | all-gather | bytes 34816 | tf_op jit(solution)/shard_map/all_gather | solution.py:105
  657.0 7.0 %multiply_add_fusion = (f32[4096,128]{0,1:T(8,128)}, f32[4096,128]{0,1:T(8,128)}) fusion(f32[4096,128]{0,1:T(8,128)} %get-tuple-element.62, f32[128]{0:T(128)S(1)} %get-tuple-element.72, f32[128]{0:T(128)S(1)} %get-tuple-element.71, f32[128]{0:T(128)S(1)} %get-tuple-element.70, f32[128]{0:T(128)S(1)} %get-tuple-element.17, ...), kind=kLoop, calls=%fused_computation.23 | loop fusion | flops 15204352 | bytes 18876416 | tf_op jit(solution)/shard_map/add | solution.py:117
  (189 shorter events, 267.2 us)
Async XLA Ops:
  7.2 160.1 %reduce-scatter.10.cloned.1.call-start = ((), (), s32[]{:S(2)}) async-start(), calls=%async_computation.3 | async-start | bytes 278528
  7.9 6.8 %collective-permute-start = (bf16[32,128]{1,0:T(8,128)(2,1)S(1)}, bf16[32,128]{1,0:T(8,128)(2,1)S(1)}, u32[]{:S(2)}, u32[]{:S(2)}) collective-permute-start(bf16[32,128]{1,0:T(8,128)(2,1)S(1)} %negate_convert_fusion), channel_id=1, source_target_pairs={{0,1},{1,2},{2,3},{3,4},{4,5},{5,6},{6,7},{7,8},{8,9},{9,10},{10,1... | collective-permute-start | bytes 24584 | tf_op jit(solution)/shard_map/ppermute | solution.py:80
  89.8 8.4 %collective-permute-start.14 = (bf16[32,128]{1,0:T(8,128)(2,1)S(1)}, bf16[32,128]{1,0:T(8,128)(2,1)S(1)}, u32[]{:S(2)}, u32[]{:S(2)}) collective-permute-start(bf16[32,128]{1,0:T(8,128)(2,1)S(1)} %collective-permute-done.13), channel_id=1, source_target_pairs={{0,1},{1,2},{2,3},{3,4},{4,5},{5,6},{6,7},{7,8},{8,9},{9,10},{10,1... | collective-permute-start | bytes 24584 | tf_op jit(solution)/shard_map/ppermute | solution.py:80
  109.7 238.9 %reduce-scatter.12.cloned.1.call-start = ((), (), s32[]{:S(2)}) async-start(), calls=%async_computation.4 | async-start | bytes 278528
  168.1 6.1 collective-permute-start.15
  174.1 6.0 collective-permute-start.16
  180.2 6.0 collective-permute-start.17
  186.2 6.0 collective-permute-start.18
  192.3 6.0 collective-permute-start.19
  198.3 6.0 collective-permute-start.20
  204.3 6.0 collective-permute-start.21
  210.4 6.0 collective-permute-start.22
  216.4 6.0 collective-permute-start.23
  222.4 6.0 collective-permute-start.24
  228.5 6.0 collective-permute-start.25
  234.5 6.0 collective-permute-start.26
  240.6 6.0 collective-permute-start.27
  246.6 6.0 collective-permute-start.28
  252.6 6.0 collective-permute-start.29
  294.1 241.5 %reduce-scatter.14.cloned.1.call-start = ((), (), s32[]{:S(2)}) async-start(), calls=%async_computation.5 | async-start | bytes 278528
  349.5 6.1 collective-permute-start.30
  355.6 6.0 collective-permute-start.31
  361.6 6.0 collective-permute-start.32
  367.7 6.0 collective-permute-start.33
  373.7 6.0 collective-permute-start.34
  379.7 6.0 collective-permute-start.35
  385.8 6.0 collective-permute-start.36
  391.8 6.0 collective-permute-start.37
  536.4 6.1 collective-permute-start.45
  548.6 6.0 collective-permute-start.47
  590.8 6.0 collective-permute-start.54
  621.0 6.0 collective-permute-start.59
  (44 other events, 423.0 us)
Sparse Core Ops, SparseCore 0:
  109.8 57.3 reduce-scatter.9
  294.3 54.3 reduce-scatter.11
  481.2 54.3 reduce-scatter.13
